TPU v7x, 256 devices: a whole 4x4x8 slice. The times are simulated.
256 devices in a mesh: fsdp: 16 (over y, z_lo, core), uly: 4 (over x), blk: 4 (over z_hi).
Axes of the slice: x: 4, y: 4, z: 8 (z_hi: 4, z_lo: 2; z = z_hi * 2 + z_lo), core: 2. Of those that a mesh axis runs over, the one named last changes fastest.
Arguments:
- latents: bfloat16 [16, 3072, 3072], P('fsdp', ('uly', 'blk')), may hold values from -40 to 40
- sampler_noise: bfloat16 [16, 3072, 3072], P('fsdp', ('uly', 'blk')), may hold values from -6 to 6
- query_key_value_weight: bfloat16 [3, 3072, 1536], P(None, 'fsdp', 'uly'), may hold values from -0.375 to 0.375
- output_weight: bfloat16 [3072, 1536], P('fsdp', 'uly'), may hold values from -0.15625 to 0.15625
- adapter_down_map: bfloat16 [64, 1536], P(None, 'uly'), may hold values from -0.15625 to 0.15625
- adapter_up_map: bfloat16 [64, 3072], replicated, may hold values from -0.75 to 0.75
- valid_token_count: int32 [16], P('fsdp'), may hold values from 1536 to 3072
- advantage: float32 [16], P('fsdp'), may hold values from -3 to 3
- timestep_index: int32 [1], replicated, may hold values from 1 to 15
Outputs:
- next_latents: bfloat16 [16, 3072, 3072], P('fsdp', ('uly', 'blk'))
- log_ratio: float32 [16], P('fsdp')
- grad_down: float32 [64, 1536], P(None, 'uly')
- grad_up: float32 [64, 3072], replicated
All inputs are finite; a program needn't handle non-finite values.
Results may differ from a plain program's by a relative error of at most 0.0055.
The roundings to bfloat16 on the way count: a program that leaves them out, or rounds other values in their place, can miss the bound.
Values may be sent and summed in bfloat16 or wider, within the bound.
No kernel may reach another device: no remote copies, remote signals or barrier semaphores. Data moves between devices by JAX's collectives and lax.ppermute only.
A program may use at most 128 MiB of HBM per device.

v0:
```python
import math
import jax
import jax.numpy as jnp
from jax import lax
from jax.sharding import PartitionSpec as P

HEAD_SIZE = 128
STEPS = 16
noise_level = 0.7
loss_scale = 4194304.0
rms_eps = 1e-06


def shards(
    latents,
    sampler_noise,
    query_key_value_weight,
    output_weight,
    adapter_down_map,
    adapter_up_map,
    valid_token_count,
    advantage,
    timestep_index,
):
    current = latents[0].astype(jnp.float32)
    rows = current.shape[0]
    width = current.shape[1]
    normed = (current * lax.rsqrt(jnp.mean(current * current, -1, keepdims=True) + rms_eps)).astype(
        jnp.bfloat16
    )
    gathered = lax.all_gather(normed, "uly", axis=0, tiled=True)
    projected = jnp.einsum(
        "td,kdh->kth",
        gathered,
        lax.all_gather(query_key_value_weight, "fsdp", axis=1, tiled=True),
        preferred_element_type=jnp.float32,
    ).astype(jnp.bfloat16)
    query_rows = projected[0]
    key_rows, value_rows = (
        lax.all_gather(projected[1], "blk", axis=0, tiled=True),
        lax.all_gather(projected[2], "blk", axis=0, tiled=True),
    )
    uly_count = lax.axis_size("uly")
    blk_count = lax.axis_size("blk")
    uly_id = lax.axis_index("uly")
    blk_id = lax.axis_index("blk")
    limit = valid_token_count[0]
    group_rows = uly_count * rows
    key_index = jnp.arange(key_rows.shape[0], dtype=jnp.int32)
    key_pos = (
        key_index % group_rows // rows * blk_count + key_index // group_rows
    ) * rows + key_index % rows
    key_ok = (key_pos < limit)[None, None, :]
    heads_here = query_rows.shape[1] // HEAD_SIZE
    query_split = query_rows.reshape(query_rows.shape[0], heads_here, HEAD_SIZE)
    key_split = key_rows.reshape(key_rows.shape[0], heads_here, HEAD_SIZE)
    value_split = value_rows.reshape(value_rows.shape[0], heads_here, HEAD_SIZE)
    scores = jnp.einsum(
        "qhd,khd->hqk", query_split, key_split, preferred_element_type=jnp.float32
    ) * (1.0 / math.sqrt(HEAD_SIZE))
    masked = jnp.where(key_ok, scores, -1e30)
    row_max = jnp.max(masked, -1, keepdims=True)
    exp_terms = jnp.where(key_ok, jnp.exp(masked - row_max), 0.0)
    weights = (exp_terms / jnp.sum(exp_terms, -1, keepdims=True)).astype(jnp.bfloat16)
    attention_output = jnp.einsum(
        "hqk,khd->qhd", weights, value_split, preferred_element_type=jnp.float32
    )
    attention_output = attention_output.astype(jnp.bfloat16).reshape(
        query_rows.shape[0], heads_here * HEAD_SIZE
    )
    weight_cols = lax.all_gather(output_weight, "fsdp", axis=0, tiled=True)
    contract_product = (((1,), (1,)), ((), ()))
    own_heads = lax.all_to_all(attention_output, "uly", split_axis=0, concat_axis=1, tiled=True)
    weight_full, down_full = (
        lax.all_gather(weight_cols, "uly", axis=1, tiled=True),
        lax.all_gather(adapter_down_map, "uly", axis=1, tiled=True),
    )
    velocity = lax.dot_general(
        own_heads, weight_full, contract_product, preferred_element_type=jnp.float32
    )
    narrow_projection = lax.dot_general(
        own_heads, down_full, contract_product, preferred_element_type=jnp.float32
    ).astype(jnp.bfloat16)
    adapter_result = jnp.dot(narrow_projection, adapter_up_map, preferred_element_type=jnp.float32)
    step_float = timestep_index[0].astype(jnp.float32)
    time_now = 1.0 - step_float / STEPS
    step_size = 1.0 / STEPS
    noise_std = noise_level * jnp.sqrt(time_now / (1.0 - time_now))
    drift_gain = 1.0 + noise_level**2 / 2.0
    ratio_gain = jnp.sqrt(step_size) * drift_gain / noise_std
    noise_f = sampler_noise[0].astype(jnp.float32)
    moved = current - step_size * (
        drift_gain * velocity + noise_level**2 * current / (2.0 * (1.0 - time_now))
    )
    next_latents = (moved + noise_std * jnp.sqrt(step_size) * noise_f).astype(jnp.bfloat16)[None]
    standard = noise_f + ratio_gain * adapter_result
    tok_pos = (uly_id * blk_count + blk_id) * rows + jnp.arange(rows, dtype=jnp.int32)
    tok_ok = (tok_pos < limit)[:, None]
    valid_len = limit.astype(jnp.float32)
    partial_log = jnp.sum(jnp.where(tok_ok, noise_f * noise_f - standard * standard, 0.0)) / (
        2.0 * valid_len * width
    )
    log_ratio = lax.psum(partial_log, ("uly", "blk"))
    coef = (
        loss_scale
        * advantage[0]
        * jnp.exp(log_ratio)
        * ratio_gain
        / (lax.axis_size("fsdp") * valid_len * width)
    )
    delta_gradient = (jnp.where(tok_ok, standard, 0.0) * coef).astype(jnp.bfloat16)
    first_axis = (((0,), (0,)), ((), ()))
    up_part = lax.dot_general(
        narrow_projection, delta_gradient, first_axis, preferred_element_type=jnp.float32
    )
    narrow_gradient = lax.dot_general(
        delta_gradient, adapter_up_map, contract_product, preferred_element_type=jnp.float32
    ).astype(jnp.bfloat16)
    down_part = lax.dot_general(
        narrow_gradient, own_heads, first_axis, preferred_element_type=jnp.float32
    )
    grad_up, down_total = lax.psum((up_part, down_part), ("fsdp", "uly", "blk"))
    local_columns = adapter_down_map.shape[1]
    grad_down = lax.dynamic_slice_in_dim(down_total, uly_id * local_columns, local_columns, 1)
    return (next_latents, jnp.reshape(log_ratio, (1,)), grad_down, grad_up)


def solution(mesh):
    placed = (
        P("fsdp", ("uly", "blk"), None),
        P("fsdp", ("uly", "blk"), None),
        P(None, "fsdp", "uly"),
        P("fsdp", "uly"),
        P(None, "uly"),
        P(),
        P("fsdp"),
        P("fsdp"),
        P(),
    )
    return jax.shard_map(
        shards,
        mesh=mesh,
        in_specs=placed,
        out_specs=(P("fsdp", ("uly", "blk"), None), P("fsdp"), P(None, "uly"), P()),
        check_vma=False,
    )
```

profile of v0, /device:TPU:1, one launch (start us, length us, event | category | flops | bytes accessed | tf_op | source)
XLA Modules:
  0.0 696.5 jit_solution(7782017306988435983)
XLA Ops:
  7.2 0.0 copy-start
  7.2 0.0 all-gather.9.cloned.1.call-start
  7.2 1.6 fusion.19
  8.9 2.6 fusion.20
  11.5 0.0 all-gather.9.cloned.1.call-update
  11.5 0.0 all-gather.11.cloned.1.call-start
  11.5 0.7 all-gather.11.cloned.1.call-update
  12.2 0.0 all-gather.19.cloned.1.call-start
  12.3 58.1 %all-gather.9.cloned.1.call-done = bf16[768,3072]{1,0:T(8,128)(2,1)} async-done(((bf16[192,3072]{1,0:T(8,128)(2,1)}), bf16[768,3072]{1,0:T(8,128)(2,1)}) %all-gather.9.cloned.1.call-update) | async-done | bytes 4718608 | tf_op jit(solution)/shard_map/all_gather | solution.py:31
  70.3 51.3 %all-gather.11.cloned.1.call-done = bf16[3,3072,384]{2,1,0:T(8,128)(2,1)} async-done(((bf16[3,192,384]{2,1,0:T(8,128)(2,1)}), bf16[3,3072,384]{2,1,0:T(8,128)(2,1)}) %all-gather.11.cloned.1.call-update) | async-done | bytes 7077904 | tf_op jit(solution)/shard_map/all_gather | solution.py:35
  121.7 10.3 %convert_bitcast_fusion = bf16[3,768,384]{1,2,0:T(8,128)(2,1)S(1)} fusion(bf16[3,3072,384]{2,1,0:T(8,128)(2,1)} %all-gather.11.cloned.1.call-done, bf16[768,3072]{1,0:T(8,128)(2,1)} %all-gather.9.cloned.1.call-done), kind=kOutput, calls=%fused_computation.33 | convolution fusion | flops 5436702720 | bytes 13565952 | tf_op jit(solution)/shard_map/td,kdh->kth/dot_general | solution.py:32
  132.0 1.1 fusion.53
  133.1 0.0 all-gather.19.cloned.1.call-update
  133.1 0.0 all-gather.17.cloned.1.call-start
  133.2 0.5 all-gather.17.cloned.1.call-update
  133.7 0.2 all-gather.13.cloned.1.call-start
  133.9 0.4 all-gather.13.cloned.1.call-update
  135.0 50.7 %all-gather.19.cloned.1.call-done = bf16[1,3072,384]{1,2,0:T(8,128)(2,1)} async-done(((bf16[1,768,384]{1,2,0:T(8,128)(2,1)}), bf16[1,3072,384]{1,2,0:T(8,128)(2,1)}) %all-gather.19.cloned.1.call-update) | async-done | bytes 2359312 | tf_op jit(solution)/shard_map/all_gather | solution.py:40
  185.6 16.2 %fusion.54 = (f32[3,768]{1,0:T(4,128)S(1)}, f32[3,768,3072]{2,1,0:T(8,128)}) fusion(pred[3072]{0:T(1024)(128)(4,1)S(1)} %fusion.47, bf16[768,3,128]{0,2,1:T(8,128)(2,1)S(1)} %bitcast.55, bf16[3072,3,128]{0,2,1:T(8,128)(2,1)} %bitcast.56), kind=kOutput, calls=%fused_computation.75 | convolution fusion | flops 1847331840 | bytes 31272960 | tf_op jit(solution)/shard_map/sub | solution.py:63
  201.9 44.3 %all-gather.17.cloned.1.call-done = bf16[1,3072,384]{1,2,0:T(8,128)(2,1)} async-done(((bf16[1,768,384]{1,2,0:T(8,128)(2,1)}), bf16[1,3072,384]{1,2,0:T(8,128)(2,1)}) %all-gather.17.cloned.1.call-update) | async-done | bytes 2359312 | tf_op jit(solution)/shard_map/all_gather | solution.py:41
  246.2 12.1 %fusion.25 = bf16[768,3,128]{0,2,1:T(8,128)(2,1)S(1)} fusion(bf16[3072,3,128]{0,2,1:T(8,128)(2,1)} %bitcast.57, f32[3,768,3072]{2,1,0:T(8,128)} %get-tuple-element.10, f32[3,768]{1,0:T(4,128)S(1)} %get-tuple-element.9), kind=kOutput, calls=%fused_computation.35 | convolution fusion | flops 1826390016 | bytes 31269888 | tf_op jit(solution)/shard_map/hqk,khd->qhd/dot_general | solution.py:65
  258.2 0.0 copy-start.3
  258.2 0.7 reshape.95
  258.9 1.4 copy.21
  260.3 3.5 all-to-all-start
  263.8 0.0 all-reduce.3.cloned.1.call-start
  265.3 0.0 copy-done.3
  265.3 12.0 %all_gather.27 = bf16[64,1536]{1,0:T(8,128)(2,1)S(1)} all-gather(bf16[64,384]{1,0:T(8,128)(2,1)S(1)} %copy-done.3), channel_id=1, replica_groups=mesh['fsdp'=16,'uly'=4,'blk'=4] {'uly'}, dimensions={1}, use_global_device_ids=true | all-gather | bytes 245760 | tf_op jit(solution)/shard_map/all_gather | solution.py:76
  277.4 0.0 all-to-all-done
  277.4 0.1 copy.22
  277.5 0.3 convolution_convert_fusion.1
  277.8 0.0 copy-done
  277.8 2.8 fusion.18
  281.2 36.3 %psum.21 = f32[]{:T(128)} all-reduce(f32[]{:T(128)S(6)} %div.64), channel_id=1, replica_groups=mesh['fsdp'=16,'uly'=4,'blk'=4] {'uly','blk'}, use_global_device_ids=true, to_apply=%region_4.5 | all-reduce | flops 1 | bytes 8 | tf_op jit(solution)/shard_map/psum | solution.py:103
  318.3 1.3 fusion.52
  319.6 1.7 fusion.26
  321.3 0.0 copy-start.1
  321.3 0.0 all-reduce.3.cloned.1.call-update
  321.3 0.0 all-gather.15.cloned.1.call-start
  321.4 0.0 all-gather.13.cloned.1.call-done
  321.4 0.7 all-gather.15.cloned.1.call-update
  322.1 262.3 %all-reduce.3.cloned.1.call-done = (f32[64,1536]{1,0:T(8,128)}, f32[64,3072]{1,0:T(8,128)}) async-done(((f32[64,1536]{1,0:T(8,128)}, f32[64,3072]{1,0:T(8,128)}), (f32[64,1536]{1,0:T(8,128)}, f32[64,3072]{1,0:T(8,128)})) %all-reduce.3.cloned.1.call-update) | async-done | bytes 1179664 | tf_op jit(solution)/shard_map/psum | solution.py:122
  584.4 1.5 constant_dynamic-slice_fusion
  586.0 94.5 %all-gather.15.cloned.1.call-done = bf16[3072,1536]{1,0:T(8,128)(2,1)} async-done(((bf16[3072,384]{1,0:T(8,128)(2,1)}), bf16[3072,1536]{1,0:T(8,128)(2,1)}) %all-gather.15.cloned.1.call-update) | async-done | bytes 9437200 | tf_op jit(solution)/shard_map/all_gather | solution.py:75
  680.5 0.0 copy-done.1
  680.5 8.3 %fusion.13 = bf16[1,192,3072]{2,1,0:T(8,128)(2,1)} fusion(bf16[192,1536]{1,0:T(8,128)(2,1)S(1)} %bitcast.53, bf16[3072,1536]{1,0:T(8,128)(2,1)} %all-gather.15.cloned.1.call-done, bf16[1,192,3072]{2,1,0:T(8,128)(2,1)} %param.10, bf16[1,192,3072]{2,1,0:T(8,128)(2,1)S(1)} %copy-done.1, f32[]{:T(128)S(6)} %mul.121, f32[]{:T(128)S(6)} %mul.118), kind=kOutput, calls=%fused_computation.22 | convolution fusion | flops 1818427392 | bytes 13565960 | tf_op jit(solution)/shard_map/dot_general | solution.py:78
  688.8 0.0 copy-done.2
  688.8 0.9 copy.28
  (4 shorter events, 0.0 us)
Async XLA Ops:
  7.2 270.6 %copy-start = (bf16[64,3072]{1,0:T(8,128)(2,1)S(1)}, bf16[64,3072]{1,0:T(8,128)(2,1)}, u32[]{:S(2)}) copy-start(bf16[64,3072]{1,0:T(8,128)(2,1)} %param.14) | copy-start | bytes 1179652
  7.2 63.2 %all-gather.9.cloned.1.call-start = ((), (), s32[]{:S(2)}) async-start(), calls=%async_computation.1 | async-start | bytes 5898240 | tf_op jit(solution)/shard_map/all_gather | solution.py:31
  11.5 110.2 %all-gather.11.cloned.1.call-start = ((), (), s32[]{:S(2)}) async-start(), calls=%async_computation.2 | async-start | bytes 7520256 | tf_op jit(solution)/shard_map/all_gather | solution.py:35
  12.2 173.4 %all-gather.19.cloned.1.call-start = ((), (), s32[]{:S(2)}) async-start(), calls=%async_computation.6 | async-start | bytes 2949120 | tf_op jit(solution)/shard_map/all_gather | solution.py:40
  133.1 113.0 %all-gather.17.cloned.1.call-start = ((), (), s32[]{:S(2)}) async-start(), calls=%async_computation.5 | async-start | bytes 2949120 | tf_op jit(solution)/shard_map/all_gather | solution.py:41
  133.7 187.7 %all-gather.13.cloned.1.call-start = ((), (), s32[]{:S(2)}) async-start(), calls=%async_computation.3 | async-start | bytes 2506752 | tf_op jit(solution)/shard_map/all_gather | solution.py:71
  258.2 7.1 %copy-start.3 = (bf16[64,384]{1,0:T(8,128)(2,1)S(1)}, bf16[64,384]{1,0:T(8,128)(2,1)}, u32[]{:S(2)}) copy-start(bf16[64,384]{1,0:T(8,128)(2,1)} %param.13) | copy-start | bytes 147460
  260.3 17.0 %all-to-all-start = ((bf16[4,192,384]{2,1,0:T(8,128)(2,1)}), bf16[4,192,384]{2,1,0:T(8,128)(2,1)S(1)}, u32[]{:S(2)}, u32[]{:S(2)}) async-start(bf16[4,192,384]{2,1,0:T(8,128)(2,1)} %copy.21), calls=%async_computation | async-start | bytes 1179648 | tf_op jit(solution)/shard_map/all_to_all | solution.py:73
  263.8 320.6 %all-reduce.3.cloned.1.call-start = ((), (), s32[]{:S(2)}) async-start(), calls=%async_computation.7 | async-start | bytes 2359296 | tf_op jit(solution)/shard_map/psum | solution.py:122
  321.3 359.2 %copy-start.1 = (bf16[1,192,3072]{2,1,0:T(8,128)(2,1)S(1)}, bf16[1,192,3072]{2,1,0:T(8,128)(2,1)}, u32[]{:S(2)}) copy-start(bf16[1,192,3072]{2,1,0:T(8,128)(2,1)} %param.9) | copy-start | bytes 3538948
  321.3 359.2 %all-gather.15.cloned.1.call-start = ((), (), s32[]{:S(2)}) async-start(), calls=%async_computation.4 | async-start | bytes 11796480 | tf_op jit(solution)/shard_map/all_gather | solution.py:75
  586.0 102.8 %copy-start.2 = (f32[64,3072]{1,0:T(8,128)S(1)}, f32[64,3072]{1,0:T(8,128)}, u32[]{:S(2)}) copy-start(f32[64,3072]{1,0:T(8,128)} %get-tuple-element.16) | copy-start | bytes 2359300
Sparse Core Ops, SparseCore 0:
  11.6 58.6 all-gather.8
  72.1 49.4 all-gather.10
  133.3 52.3 all-gather.18
  187.9 58.2 all-gather.16
  247.8 35.5 all-gather.12
  321.4 262.9 all-reduce.2
  586.3 94.2 all-gather.14
where the time goes:
time: 697 us
  waiting for transfers between devices  564 us (81%)
  matrix products  53 us (8%)
  blocking collectives  48.4 us (7%)
  between operations  17.7 us (3%)
    psum x1, waiting for transfers between devices, shards(): grad_up, down_total = lax.psum((up_part, down_part), ('fsdp', 'uly', 'blk'))  262 us
    all_gather x1, waiting for transfers between devices, shards(): lax.all_gather(weight_cols, 'uly', axis=1, tiled=True)  94.5 us
    all_gather x1, waiting for transfers between devices, shards(): gathered = lax.all_gather(normed, 'uly', axis=0, tiled=True)  58.1 us
    all_gather x1, waiting for transfers between devices, shards(): lax.all_gather(query_key_value_weight, 'fsdp', axis=1, tiled=True)  51.3 us
    all_gather x1, waiting for transfers between devices, shards(): lax.all_gather(projected[1], 'blk', axis=0, tiled=True)  50.7 us
    all_gather x1, waiting for transfers between devices, shards(): lax.all_gather(projected[2], 'blk', axis=0, tiled=True)  44.3 us
    psum x1, blocking collectives, shards(): log_ratio = lax.psum(partial_log, ('uly', 'blk'))  36.3 us
    sub x1, matrix products, shards(): exp_terms = jnp.where(key_ok, jnp.exp(masked - row_max), 0.0)  16.2 us
  transfers between devices with their start and end apart: 8, of which 6 were waited for; matrix products, arithmetic and copies ran while one was open for 5% of the time, Pallas kernels for 0%

commit v1 on v0

--- a/solution.py
+++ b/solution.py
@@ -1,3 +1,4 @@
+import functools
 import math
 import jax
 import jax.numpy as jnp
@@ -9,6 +10,16 @@
 noise_level = 0.7
 loss_scale = 4194304.0
 rms_eps = 1e-06
+
+
+def load_stocks(shard_in, net_axis, array_dim):
+    return jnp.concatenate(
+        lax.all_to_all(jnp.stack([shard_in] * lax.axis_size(net_axis), 0), net_axis, 0, 0),
+        array_dim,
+    )
+
+
+mix_the_values = functools.partial(load_stocks, net_axis="uly", array_dim=1)
 
 
 def shards(
@@ -72,7 +83,7 @@
     contract_product = (((1,), (1,)), ((), ()))
     own_heads = lax.all_to_all(attention_output, "uly", split_axis=0, concat_axis=1, tiled=True)
     weight_full, down_full = (
-        lax.all_gather(weight_cols, "uly", axis=1, tiled=True),
+        mix_the_values(weight_cols),
         lax.all_gather(adapter_down_map, "uly", axis=1, tiled=True),
     )
     velocity = lax.dot_general(

time: 697 us -> 724 us (1.039)
  blocking collectives: 48.4 us -> 146 us
  waiting for transfers between devices: 564 us -> 478 us
  local copies, waits for them, and re-layouts: 5.72 us -> 13.2 us
    all_gather x1, blocking collectives: 12 us -> 107 us  [shards(): lax.all_gather(adapter_down_map, 'uly', axis=1, tiled=True)]
    all_gather x1 -> x0, waiting for transfers between devices: 94.5 us -> none  [shards(): lax.all_gather(weight_cols, 'uly', axis=1, tiled=True)]
    all_gather x1, waiting for transfers between devices: 0.02 us -> 19.6 us  [shards(): weight_cols = lax.all_gather(output_weight, 'fsdp', axis=0, tiled=True)]
    psum x1, waiting for transfers between devices: 262 us -> 252 us  [shards(): grad_up, down_total = lax.psum((up_part, down_part), ('fsdp', 'uly', 'blk'))]
  transfers between devices with their start and end apart: 8 -> 8, of which waited for: 6 -> 6; matrix products, arithmetic and copies ran while one was open for 5% -> 6% of each run, Pallas kernels for 0% -> 0%
where the time goes in v1:
time: 724 us; the launch traced here: 722 us
  waiting for transfers between devices  478 us (66%)
  blocking collectives  146 us (20%)
  matrix products  53.5 us (7%)
  between operations  17.7 us (2%)
  local copies, waits for them, and re-layouts  13.2 us (2%)
  starting transfers between devices  9.84 us (1%)
    psum x1, waiting for transfers between devices, shards(): grad_up, down_total = lax.psum((up_part, down_part), ('fsdp', 'uly', 'blk'))  252 us
    all_gather x1, blocking collectives, shards(): lax.all_gather(adapter_down_map, 'uly', axis=1, tiled=True)  107 us
    all_gather x1, waiting for transfers between devices, shards(): gathered = lax.all_gather(normed, 'uly', axis=0, tiled=True)  58.1 us
    all_gather x1, waiting for transfers between devices, shards(): lax.all_gather(query_key_value_weight, 'fsdp', axis=1, tiled=True)  51.3 us
    all_gather x1, waiting for transfers between devices, shards(): lax.all_gather(projected[1], 'blk', axis=0, tiled=True)  50.7 us
    all_gather x1, waiting for transfers between devices, shards(): lax.all_gather(projected[2], 'blk', axis=0, tiled=True)  44.3 us
    psum x1, blocking collectives, shards(): log_ratio = lax.psum(partial_log, ('uly', 'blk'))  38.5 us
    all_gather x1, waiting for transfers between devices, shards(): weight_cols = lax.all_gather(output_weight, 'fsdp', axis=0, tiled=True)  19.6 us
  transfers between devices with their start and end apart: 8, of which 6 were waited for; matrix products, arithmetic and copies ran while one was open for 6% of the time, Pallas kernels for 0%

profile of v1, /device:TPU:1, one launch (start us, length us, event | category | flops | bytes accessed | tf_op | source)
XLA Modules:
  0.0 721.8 jit_solution(12990748892763849995)
XLA Ops:
  7.2 0.0 copy-start
  7.2 0.0 all-gather.8.cloned.1.call-start
  7.2 1.6 fusion.39
  8.9 2.6 fusion.40
  11.5 0.0 all-gather.8.cloned.1.call-update
  11.5 0.0 all-gather.10.cloned.1.call-start
  11.5 0.7 all-gather.10.cloned.1.call-update
  12.2 0.0 all-gather.16.cloned.1.call-start
  12.3 58.1 %all-gather.8.cloned.1.call-done = bf16[768,3072]{1,0:T(8,128)(2,1)} async-done(((bf16[192,3072]{1,0:T(8,128)(2,1)}), bf16[768,3072]{1,0:T(8,128)(2,1)}) %all-gather.8.cloned.1.call-update) | async-done | bytes 4718608 | tf_op jit(solution)/shard_map/all_gather | solution.py:42
  70.3 51.3 %all-gather.10.cloned.1.call-done = bf16[3,3072,384]{2,1,0:T(8,128)(2,1)} async-done(((bf16[3,192,384]{2,1,0:T(8,128)(2,1)}), bf16[3,3072,384]{2,1,0:T(8,128)(2,1)}) %all-gather.10.cloned.1.call-update) | async-done | bytes 7077904 | tf_op jit(solution)/shard_map/all_gather | solution.py:46
  121.7 10.3 %convert_bitcast_fusion = bf16[3,768,384]{1,2,0:T(8,128)(2,1)S(1)} fusion(bf16[3,3072,384]{2,1,0:T(8,128)(2,1)} %all-gather.10.cloned.1.call-done, bf16[768,3072]{1,0:T(8,128)(2,1)} %all-gather.8.cloned.1.call-done), kind=kOutput, calls=%fused_computation.36 | convolution fusion | flops 5436702720 | bytes 13565952 | tf_op jit(solution)/shard_map/td,kdh->kth/dot_general | solution.py:43
  132.0 1.1 fusion.74
  133.1 0.0 all-gather.16.cloned.1.call-update
  133.1 0.0 all-gather.14.cloned.1.call-start
  133.2 0.5 all-gather.14.cloned.1.call-update
  133.7 0.2 all-gather.12.cloned.1.call-start
  133.9 0.4 all-gather.12.cloned.1.call-update
  135.0 50.7 %all-gather.16.cloned.1.call-done = bf16[1,3072,384]{1,2,0:T(8,128)(2,1)} async-done(((bf16[1,768,384]{1,2,0:T(8,128)(2,1)}), bf16[1,3072,384]{1,2,0:T(8,128)(2,1)}) %all-gather.16.cloned.1.call-update) | async-done | bytes 2359312 | tf_op jit(solution)/shard_map/all_gather | solution.py:51
  185.6 16.2 %fusion.75 = (f32[3,768]{1,0:T(4,128)S(1)}, f32[3,768,3072]{2,1,0:T(8,128)}) fusion(pred[3072]{0:T(1024)(128)(4,1)S(1)} %fusion.68, bf16[768,3,128]{0,2,1:T(8,128)(2,1)S(1)} %bitcast.89, bf16[3072,3,128]{0,2,1:T(8,128)(2,1)} %bitcast.90), kind=kOutput, calls=%fused_computation.79 | convolution fusion | flops 1847331840 | bytes 31272960 | tf_op jit(solution)/shard_map/sub | solution.py:74
  201.9 44.3 %all-gather.14.cloned.1.call-done = bf16[1,3072,384]{1,2,0:T(8,128)(2,1)} async-done(((bf16[1,768,384]{1,2,0:T(8,128)(2,1)}), bf16[1,3072,384]{1,2,0:T(8,128)(2,1)}) %all-gather.14.cloned.1.call-update) | async-done | bytes 2359312 | tf_op jit(solution)/shard_map/all_gather | solution.py:52
  246.2 12.1 %fusion.45 = bf16[768,3,128]{0,2,1:T(8,128)(2,1)S(1)} fusion(bf16[3072,3,128]{0,2,1:T(8,128)(2,1)} %bitcast.91, f32[3,768,3072]{2,1,0:T(8,128)} %get-tuple-element.10, f32[3,768]{1,0:T(4,128)S(1)} %get-tuple-element.9), kind=kOutput, calls=%fused_computation.38 | convolution fusion | flops 1826390016 | bytes 31269888 | tf_op jit(solution)/shard_map/hqk,khd->qhd/dot_general | solution.py:76
  258.2 0.7 reshape.103
  258.9 1.4 copy.22
  260.3 3.5 all-to-all-start
  263.8 19.6 %all-gather.12.cloned.1.call-done = bf16[3072,384]{1,0:T(8,128)(2,1)} async-done(((bf16[192,384]{1,0:T(8,128)(2,1)}), bf16[3072,384]{1,0:T(8,128)(2,1)}) %all-gather.12.cloned.1.call-update) | async-done | bytes 2359312 | tf_op jit(solution)/shard_map/all_gather | solution.py:82
  283.5 0.0 all-to-all-done
  283.5 0.0 copy-start.1
  283.5 6.3 stack.2
  289.8 0.0 copy-start.2
  289.8 5.9 all-to-all-start.1
  295.8 0.0 all-reduce.3.cloned.1.call-start
  297.2 0.0 copy-done.2
  297.3 107.0 %all_gather.23 = bf16[64,1536]{1,0:T(8,128)(2,1)S(1)} all-gather(bf16[64,384]{1,0:T(8,128)(2,1)S(1)} %copy-done.2), channel_id=1, replica_groups=mesh['fsdp'=16,'uly'=4,'blk'=4] {'uly'}, dimensions={1}, use_global_device_ids=true | all-gather | bytes 245760 | tf_op jit(solution)/shard_map/all_gather | solution.py:87
  404.3 0.0 copy-done.1
  404.3 0.1 copy.23
  404.3 0.3 convolution_convert_fusion.1
  404.6 0.0 copy-done
  404.6 2.8 fusion.38
  408.1 38.5 %psum.21 = f32[]{:T(128)} all-reduce(f32[]{:T(128)S(6)} %div.64), channel_id=1, replica_groups=mesh['fsdp'=16,'uly'=4,'blk'=4] {'uly','blk'}, use_global_device_ids=true, to_apply=%region_4.5 | all-reduce | flops 1 | bytes 8 | tf_op jit(solution)/shard_map/psum | solution.py:114
  447.4 1.3 fusion.73
  448.7 1.7 fusion.46
  450.4 0.0 all-reduce.3.cloned.1.call-update
  450.4 0.0 all-to-all-done.1
  450.4 8.8 %fusion.31 = bf16[1,192,3072]{2,1,0:T(8,128)(2,1)} fusion(bf16[4,3072,384]{2,1,0:T(8,128)(2,1)} %all-to-all-done.1, bf16[1,192,3072]{2,1,0:T(8,128)(2,1)} %param.10, bf16[1,192,3072]{2,1,0:T(8,128)(2,1)} %param.9, f32[]{:T(128)S(6)} %mul.121, f32[]{:T(128)S(6)} %mul.118, bf16[4,192,384]{2,1,0:T(8,128)(2,1)} %copy-done.1), kind=kOutput, calls=%fused_computation.25 | convolution fusion | flops 1818427392 | bytes 13565960 | tf_op jit(solution)/shard_map/dot_general | solution.py:89
  459.2 252.1 %all-reduce.3.cloned.1.call-done = (f32[64,1536]{1,0:T(8,128)}, f32[64,3072]{1,0:T(8,128)}) async-done(((f32[64,1536]{1,0:T(8,128)}, f32[64,3072]{1,0:T(8,128)}), (f32[64,1536]{1,0:T(8,128)}, f32[64,3072]{1,0:T(8,128)})) %all-reduce.3.cloned.1.call-update) | async-done | bytes 1179664 | tf_op jit(solution)/shard_map/psum | solution.py:133
  711.3 1.5 constant_dynamic-slice_fusion
  712.9 2.1 copy.29
  (3 shorter events, 0.0 us)
Async XLA Ops:
  7.2 397.5 %copy-start = (bf16[64,3072]{1,0:T(8,128)(2,1)S(1)}, bf16[64,3072]{1,0:T(8,128)(2,1)}, u32[]{:S(2)}) copy-start(bf16[64,3072]{1,0:T(8,128)(2,1)} %param.14) | copy-start | bytes 1179652
  7.2 63.2 %all-gather.8.cloned.1.call-start = ((), (), s32[]{:S(2)}) async-start(), calls=%async_computation.2 | async-start | bytes 5898240 | tf_op jit(solution)/shard_map/all_gather | solution.py:42
  11.5 110.2 %all-gather.10.cloned.1.call-start = ((), (), s32[]{:S(2)}) async-start(), calls=%async_computation.3 | async-start | bytes 7520256 | tf_op jit(solution)/shard_map/all_gather | solution.py:46
  12.2 173.4 %all-gather.16.cloned.1.call-start = ((), (), s32[]{:S(2)}) async-start(), calls=%async_computation.6 | async-start | bytes 2949120 | tf_op jit(solution)/shard_map/all_gather | solution.py:51
  133.1 113.0 %all-gather.14.cloned.1.call-start = ((), (), s32[]{:S(2)}) async-start(), calls=%async_computation.5 | async-start | bytes 2949120 | tf_op jit(solution)/shard_map/all_gather | solution.py:52
  133.7 149.7 %all-gather.12.cloned.1.call-start = ((), (), s32[]{:S(2)}) async-start(), calls=%async_computation.4 | async-start | bytes 2506752 | tf_op jit(solution)/shard_map/all_gather | solution.py:82
  260.3 23.1 %all-to-all-start = ((bf16[4,192,384]{2,1,0:T(8,128)(2,1)}), bf16[4,192,384]{2,1,0:T(8,128)(2,1)S(1)}, u32[]{:S(2)}, u32[]{:S(2)}) async-start(bf16[4,192,384]{2,1,0:T(8,128)(2,1)} %copy.22), calls=%async_computation | async-start | bytes 1179648 | tf_op jit(solution)/shard_map/all_to_all | solution.py:84
  283.5 120.8 %copy-start.1 = (bf16[4,192,384]{2,1,0:T(8,128)(2,1)}, bf16[4,192,384]{2,1,0:T(8,128)(2,1)S(1)}, u32[]{:S(2)}) copy-start(bf16[4,192,384]{2,1,0:T(8,128)(2,1)S(1)} %all-to-all-done) | copy-start | bytes 1769476
  289.8 7.4 %copy-start.2 = (bf16[64,384]{1,0:T(8,128)(2,1)S(1)}, bf16[64,384]{1,0:T(8,128)(2,1)}, u32[]{:S(2)}) copy-start(bf16[64,384]{1,0:T(8,128)(2,1)} %param.13) | copy-start | bytes 147460
  289.8 160.6 %all-to-all-start.1 = ((bf16[4,3072,384]{2,1,0:T(8,128)(2,1)}), bf16[4,3072,384]{2,1,0:T(8,128)(2,1)}, u32[]{:S(2)}, u32[]{:S(2)}) async-start(bf16[4,3072,384]{2,1,0:T(8,128)(2,1)} %stack.2), calls=%async_computation.1 | async-start | bytes 18874368 | tf_op jit(solution)/shard_map/all_to_all | solution.py:17
  295.8 415.6 %all-reduce.3.cloned.1.call-start = ((), (), s32[]{:S(2)}) async-start(), calls=%async_computation.7 | async-start | bytes 2359296 | tf_op jit(solution)/shard_map/psum | solution.py:133
Sparse Core Ops, SparseCore 0:
  11.6 58.6 all-gather.7
  72.1 49.4 all-gather.9
  133.3 52.3 all-gather.15
  187.9 58.2 all-gather.13
  247.8 35.5 all-gather.11
  450.5 260.7 all-reduce.2
